TPU v7x, 32 devices: a whole 2x2x4 slice. The times are simulated.
32 devices in a mesh: dp: 16 (over z, y, core), ctx: 2 (over x).
Axes of the slice: x: 2, y: 2, z: 4, core: 2. Of those that a mesh axis runs over, the one named last changes fastest.
Arguments:
- conv_input: bfloat16 [16, 256, 4096], P('dp', 'ctx'), may hold values from -6 to 6
- gate_value: bfloat16 [16, 256, 4096], P('dp', 'ctx'), may hold values from -6 to 6
- out_grad: bfloat16 [16, 256, 4096], P('dp', 'ctx'), may hold values from -6 to 6
- filter_taps: bfloat16 [128, 4096], P('dp'), may hold values from -0.5 to 0.5
Outputs:
- input_grad: bfloat16 [16, 256, 4096], P('dp', 'ctx')
- filter_grad: float32 [128, 4096], P('dp')
All inputs are finite; a program needn't handle non-finite values.
Results may differ from a plain program's by a relative error of at most 0.0051.
Values may be sent and summed in bfloat16 or wider, within the bound.
A program may use at most 64 MiB of HBM per device.

v0:
```python
import math
import jax
import jax.numpy as jnp
from jax import lax
from jax.sharding import PartitionSpec as P

TAPS = 128


def from_behind(block, axis, distance):
    devices = range(lax.axis_size(axis))
    route = [(i - distance, i) for i in devices if i - distance in devices]
    return lax.ppermute(block, axis, route)


def correlate(signal, kernel):
    return lax.conv_general_dilated(
        signal[None],
        kernel[:, None, :],
        (1,),
        "VALID",
        dimension_numbers=("NWC", "WIO", "NWC"),
        feature_group_count=signal.shape[1],
        preferred_element_type=jnp.float32,
    )[0]


def shards(conv_input, gate_value, out_grad, filter_taps):
    inputs = conv_input[0]
    rows = inputs.shape[0]
    mixed = (out_grad[0].astype(jnp.float32) * gate_value[0].astype(jnp.float32)).astype(
        jnp.bfloat16
    )
    rim_rows = from_behind(mixed[: TAPS - 1], "ctx", -1)
    grad_ext = jnp.concatenate([mixed, rim_rows], 0)
    partial_grad = correlate(grad_ext, inputs)
    full_taps = lax.all_gather(filter_taps, "dp", axis=0, tiled=True)
    back_sum = correlate(grad_ext, full_taps)
    summed = lax.psum(partial_grad, "ctx")
    shard_grad = lax.psum_scatter(summed, "dp", scatter_dimension=0, tiled=True)
    tokens_all = rows * lax.axis_size("ctx") * lax.axis_size("dp")
    scale_factor = 1.0 / math.sqrt(tokens_all)
    return (back_sum.astype(jnp.bfloat16)[None], shard_grad * scale_factor)


def solution(mesh):
    in_specs = (P("dp", "ctx", None), P("dp", "ctx", None), P("dp", "ctx", None), P("dp", None))
    out_specs = (P("dp", "ctx", None), P("dp", None))
    return jax.shard_map(shards, mesh=mesh, in_specs=in_specs, out_specs=out_specs, check_vma=False)
```

profile of v0, /device:TPU:0, one launch (start us, length us, event | category | flops | bytes accessed | tf_op | source)
XLA Modules:
  0.0 211.5 jit_solution(7849527368872966788)
XLA Ops:
  7.2 0.0 copy-start
  7.2 0.0 reduce-scatter.2.cloned.1.call-start
  7.2 1.9 multiply_convert_fusion
  9.2 0.1 slice_bitcast_fusion
  9.2 1.3 collective-permute-start
  10.5 26.2 %collective-permute-done = bf16[127,4096]{1,0:T(8,128)(2,1)S(1)} collective-permute-done((bf16[127,4096]{1,0:T(8,128)(2,1)S(1)}, bf16[127,4096]{1,0:T(8,128)(2,1)S(1)}, u32[]{:S(2)}, u32[]{:S(2)}) %collective-permute-start) | collective-permute-done | bytes 1040416 | tf_op jit(solution)/shard_map/ppermute | solution.py:13
  36.7 0.2 maximum_bitcast_fusion
  36.9 0.0 copy-done
  36.9 30.1 %fusion = f32[1,128,4096]{2,0,1:T(1,128)S(1)} fusion(bf16[1,255,4096]{2,1,0:T(8,128)(2,1)S(1)} %maximum_bitcast_fusion, bf16[128,1,4096]{2,0,1:T(8,128)(2,1)S(1)} %bitcast.10), kind=kOutput, calls=%fused_computation.1 | convolution fusion | flops 134217728 | bytes 5234688 | tf_op jit(solution)/shard_map/conv_general_dilated | solution.py:17
  67.0 3.0 %copy.23 = f32[1,128,4096]{2,1,0:T(8,128)} copy(f32[1,128,4096]{2,0,1:T(1,128)S(1)} %fusion) | data formatting | bytes 4194304
  70.0 0.0 reduce-scatter.2.cloned.1.call-update
  70.0 0.0 all-gather.2.cloned.1.call-start
  70.1 0.7 all-gather.2.cloned.1.call-update
  70.8 0.0 all-reduce.2.cloned.1.call-start
  70.8 62.3 %reduce-scatter.2.cloned.1.call-done = f32[8,4096]{1,0:T(8,128)} async-done(((f32[128,4096]{1,0:T(8,128)}), f32[8,4096]{1,0:T(8,128)}) %reduce-scatter.2.cloned.1.call-update) | async-done | bytes 131088 | tf_op jit(solution)/shard_map/reduce_scatter | solution.py:40
  133.1 0.0 all-reduce.2.cloned.1.call-update
  133.2 39.0 %all-gather.2.cloned.1.call-done = bf16[128,4096]{1,0:T(8,128)(2,1)} async-done(((bf16[8,4096]{1,0:T(8,128)(2,1)}), bf16[128,4096]{1,0:T(8,128)(2,1)}) %all-gather.2.cloned.1.call-update) | async-done | bytes 1048592 | tf_op jit(solution)/shard_map/all_gather | solution.py:37
  172.2 29.1 %convolution_convert_fusion = bf16[1,128,4096]{2,0,1:T(2,128)(2,1)S(1)} fusion(bf16[1,255,4096]{2,1,0:T(8,128)(2,1)S(1)} %maximum_bitcast_fusion, bf16[128,1,4096]{2,0,1:T(8,128)(2,1)} %bitcast.13), kind=kOutput, calls=%fused_computation | convolution fusion | flops 134742016 | bytes 4186112 | tf_op jit(solution)/shard_map/conv_general_dilated | solution.py:17
  201.3 2.1 copy.12
  203.4 0.0 all-reduce.2.cloned.1.call-done
  203.4 1.6 broadcast_multiply_fusion
Async XLA Ops:
  7.2 29.8 %copy-start = (bf16[1,128,4096]{2,1,0:T(8,128)(2,1)S(1)}, bf16[1,128,4096]{2,1,0:T(8,128)(2,1)}, u32[]{:S(2)}) copy-start(bf16[1,128,4096]{2,1,0:T(8,128)(2,1)} %param.4) | copy-start | bytes 3145732
  7.2 126.0 %reduce-scatter.2.cloned.1.call-start = ((), (), s32[]{:S(2)}) async-start(), calls=%async_computation.2 | async-start | bytes 2228224 | tf_op jit(solution)/shard_map/reduce_scatter | solution.py:40
  9.2 27.5 %collective-permute-start = (bf16[127,4096]{1,0:T(8,128)(2,1)S(1)}, bf16[127,4096]{1,0:T(8,128)(2,1)S(1)}, u32[]{:S(2)}, u32[]{:S(2)}) collective-permute-start(bf16[127,4096]{1,0:T(8,128)(2,1)S(1)} %slice_bitcast_fusion), channel_id=1, source_target_pairs={{1,0},{3,2},{5,4},{7,6},{9,8},{11,10},{13,12},{15,14},{17,16},{19,... | collective-permute-start | bytes 3121160 | tf_op jit(solution)/shard_map/ppermute | solution.py:13
  70.0 102.1 %all-gather.2.cloned.1.call-start = ((), (), s32[]{:S(2)}) async-start(), calls=%async_computation.1 | async-start | bytes 1114112 | tf_op jit(solution)/shard_map/all_gather | solution.py:37
  70.8 132.6 %all-reduce.2.cloned.1.call-start = ((), (), s32[]{:S(2)}) async-start(), calls=%async_computation.3 | async-start | bytes 262144 | tf_op jit(solution)/shard_map/psum | solution.py:39
Sparse Core Ops, SparseCore 0:
  70.2 62.9 reduce-scatter.1
  135.3 36.8 all-gather.1
  174.4 20.4 all-reduce.1
where the time goes:
time: 212 us; the launch traced here: 211 us
  waiting for transfers between devices  128 us (60%)
  matrix products  59.2 us (28%)
  between operations  13.8 us (7%)
  local copies, waits for them, and re-layouts  5.18 us (2%)
  other arithmetic  3.71 us (2%)
    reduce_scatter x1, waiting for transfers between devices, shards(): shard_grad = lax.psum_scatter(summed, 'dp', scatter_dimension=0, tiled=True)  62.3 us
    conv_general_dilated x2, matrix products, correlate(): lax.conv_general_dilated(signal[None], kernel[:, None, :], (1,), 'VALID',...  59.2 us
    all_gather x1, waiting for transfers between devices, shards(): full_taps = lax.all_gather(filter_taps, 'dp', axis=0, tiled=True)  39 us
    ppermute x1, waiting for transfers between devices, from_behind(): return lax.ppermute(block, axis, route)  26.2 us
    unnamed x4, local copies, waits for them, and re-layouts  5.1 us
  transfers between devices with their start and end apart: 4, of which 3 were waited for; matrix products, arithmetic and copies ran while one was open for 15% of the time, Pallas kernels for 0%

commit v1 on v0

--- a/solution.py
+++ b/solution.py
@@ -34,7 +34,10 @@
     rim_rows = from_behind(mixed[: TAPS - 1], "ctx", -1)
     grad_ext = jnp.concatenate([mixed, rim_rows], 0)
     partial_grad = correlate(grad_ext, inputs)
-    full_taps = lax.all_gather(filter_taps, "dp", axis=0, tiled=True)
+    passed = lax.axis_size("dp")
+    e_next = jnp.stack(passed * [filter_taps])
+    mid_arr = lax.all_to_all(e_next, "dp", 0, 0)
+    full_taps = jnp.concatenate(mid_arr, axis=0)
     back_sum = correlate(grad_ext, full_taps)
     summed = lax.psum(partial_grad, "ctx")
     shard_grad = lax.psum_scatter(summed, "dp", scatter_dimension=0, tiled=True)

time: 212 us -> 174 us (0.82)
  waiting for transfers between devices: 128 us -> 81.8 us
  starting transfers between devices: 1.41 us -> 8.18 us
    all_gather x1 -> x0, waiting for transfers between devices: 39 us -> none  [shards(): full_taps = lax.all_gather(filter_taps, 'dp', axis=0, tiled=True)]
    all_to_all x0 -> x1, starting transfers between devices: none -> 6.81 us  [shards(): mid_arr = lax.all_to_all(e_next, 'dp', 0, 0)]
    reduce_scatter x1, waiting for transfers between devices: 62.3 us -> 55.6 us  [shards(): shard_grad = lax.psum_scatter(summed, 'dp', scatter_dimension=0, tiled=True)]
    unnamed x4 -> x6, local copies, waits for them, and re-layouts: 5.1 us -> 5.91 us
  transfers between devices with their start and end apart: 4 -> 4, of which waited for: 3 -> 2; matrix products, arithmetic and copies ran while one was open for 15% -> 19% of each run, Pallas kernels for 0% -> 0%
where the time goes in v1:
time: 174 us
  waiting for transfers between devices  81.8 us (47%)
  matrix products  59.2 us (34%)
  between operations  14.1 us (8%)
  starting transfers between devices  8.18 us (5%)
  local copies, waits for them, and re-layouts  7.06 us (4%)
  other arithmetic  3.71 us (2%)
    conv_general_dilated x2, matrix products, correlate(): lax.conv_general_dilated(signal[None], kernel[:, None, :], (1,), 'VALID',...  59.2 us
    reduce_scatter x1, waiting for transfers between devices, shards(): shard_grad = lax.psum_scatter(summed, 'dp', scatter_dimension=0, tiled=True)  55.6 us
    ppermute x1, waiting for transfers between devices, from_behind(): return lax.ppermute(block, axis, route)  26.2 us
    all_to_all x1, starting transfers between devices, shards(): mid_arr = lax.all_to_all(e_next, 'dp', 0, 0)  6.81 us
    unnamed x6, local copies, waits for them, and re-layouts  5.91 us
  transfers between devices with their start and end apart: 4, of which 2 were waited for; matrix products, arithmetic and copies ran while one was open for 19% of the time, Pallas kernels for 0%

profile of v1, /device:TPU:0, one launch (start us, length us, event | category | flops | bytes accessed | tf_op | source)
XLA Modules:
  0.0 174.0 jit_solution(12907940087298782318)
XLA Ops:
  7.2 0.0 copy-start
  7.2 0.0 reduce-scatter.2.cloned.1.call-start
  7.2 1.9 %multiply_convert_fusion = bf16[1,128,4096]{2,1,0:T(8,128)(2,1)S(1)} fusion(bf16[1,128,4096]{2,1,0:T(8,128)(2,1)} %param.5, bf16[1,128,4096]{2,1,0:T(8,128)(2,1)} %param.6), kind=kLoop, calls=%fused_computation.8 | loop fusion | flops 2097152 | bytes 3145728 | tf_op jit(solution)/shard_map/convert_element_type | solution.py:31
  9.2 0.1 slice_bitcast_fusion
  9.2 1.3 collective-permute-start
  10.5 26.2 %collective-permute-done = bf16[127,4096]{1,0:T(8,128)(2,1)S(1)} collective-permute-done((bf16[127,4096]{1,0:T(8,128)(2,1)S(1)}, bf16[127,4096]{1,0:T(8,128)(2,1)S(1)}, u32[]{:S(2)}, u32[]{:S(2)}) %collective-permute-start) | collective-permute-done | bytes 1040416 | tf_op jit(solution)/shard_map/ppermute | solution.py:13
  36.7 0.2 maximum_bitcast_fusion
  36.9 0.0 copy-done
  36.9 30.1 %fusion = f32[1,128,4096]{2,0,1:T(1,128)S(1)} fusion(bf16[1,255,4096]{2,1,0:T(8,128)(2,1)S(1)} %maximum_bitcast_fusion, bf16[128,1,4096]{2,0,1:T(8,128)(2,1)S(1)} %bitcast.10), kind=kOutput, calls=%fused_computation.1 | convolution fusion | flops 134217728 | bytes 5234688 | tf_op jit(solution)/shard_map/conv_general_dilated | solution.py:17
  67.0 3.0 %copy.23 = f32[1,128,4096]{2,1,0:T(8,128)} copy(f32[1,128,4096]{2,0,1:T(1,128)S(1)} %fusion) | data formatting | bytes 4194304
  70.0 0.0 copy-start.1
  70.0 0.0 reduce-scatter.2.cloned.1.call-update
  70.1 0.8 copy-done.1
  70.9 1.1 stack.2
  71.9 6.8 %all-to-all-start = ((bf16[16,8,4096]{2,1,0:T(8,128)(2,1)}), bf16[16,8,4096]{2,1,0:T(8,128)(2,1)}, u32[]{:S(2)}, u32[]{:S(2)}) async-start(bf16[16,8,4096]{2,1,0:T(8,128)(2,1)} %stack.2), calls=%async_computation | async-start | bytes 2097152 | tf_op jit(solution)/shard_map/all_to_all | solution.py:39
  78.8 0.0 all-reduce.2.cloned.1.call-start
  78.8 55.6 %reduce-scatter.2.cloned.1.call-done = f32[8,4096]{1,0:T(8,128)} async-done(((f32[128,4096]{1,0:T(8,128)}), f32[8,4096]{1,0:T(8,128)}) %reduce-scatter.2.cloned.1.call-update) | async-done | bytes 131088 | tf_op jit(solution)/shard_map/reduce_scatter | solution.py:43
  134.4 0.0 all-reduce.2.cloned.1.call-update
  134.4 0.0 all-to-all-done
  134.4 29.1 %convolution_convert_fusion = bf16[1,128,4096]{2,0,1:T(2,128)(2,1)S(1)} fusion(bf16[1,255,4096]{2,1,0:T(8,128)(2,1)S(1)} %maximum_bitcast_fusion, bf16[128,1,4096]{2,0,1:T(8,128)(2,1)} %bitcast.3), kind=kOutput, calls=%fused_computation | convolution fusion | flops 134742016 | bytes 4186112 | tf_op jit(solution)/shard_map/conv_general_dilated | solution.py:17
  163.5 2.1 %copy.12 = bf16[1,128,4096]{2,1,0:T(8,128)(2,1)} copy(bf16[1,128,4096]{2,0,1:T(2,128)(2,1)S(1)} %convolution_convert_fusion) | data formatting | bytes 2097152
  165.6 0.0 all-reduce.2.cloned.1.call-done
  165.6 1.6 broadcast_multiply_fusion
Async XLA Ops:
  7.2 29.8 %copy-start = (bf16[1,128,4096]{2,1,0:T(8,128)(2,1)S(1)}, bf16[1,128,4096]{2,1,0:T(8,128)(2,1)}, u32[]{:S(2)}) copy-start(bf16[1,128,4096]{2,1,0:T(8,128)(2,1)} %param.4) | copy-start | bytes 3145732
  7.2 127.2 %reduce-scatter.2.cloned.1.call-start = ((), (), s32[]{:S(2)}) async-start(), calls=%async_computation.2 | async-start | bytes 2228224 | tf_op jit(solution)/shard_map/reduce_scatter | solution.py:43
  9.2 27.5 %collective-permute-start = (bf16[127,4096]{1,0:T(8,128)(2,1)S(1)}, bf16[127,4096]{1,0:T(8,128)(2,1)S(1)}, u32[]{:S(2)}, u32[]{:S(2)}) collective-permute-start(bf16[127,4096]{1,0:T(8,128)(2,1)S(1)} %slice_bitcast_fusion), channel_id=1, source_target_pairs={{1,0},{3,2},{5,4},{7,6},{9,8},{11,10},{13,12},{15,14},{17,16},{19,... | collective-permute-start | bytes 3121160 | tf_op jit(solution)/shard_map/ppermute | solution.py:13
  70.0 0.8 copy-start.1
  71.9 62.5 %all-to-all-start = ((bf16[16,8,4096]{2,1,0:T(8,128)(2,1)}), bf16[16,8,4096]{2,1,0:T(8,128)(2,1)}, u32[]{:S(2)}, u32[]{:S(2)}) async-start(bf16[16,8,4096]{2,1,0:T(8,128)(2,1)} %stack.2), calls=%async_computation | async-start | bytes 2097152 | tf_op jit(solution)/shard_map/all_to_all | solution.py:39
  78.8 86.9 %all-reduce.2.cloned.1.call-start = ((), (), s32[]{:S(2)}) async-start(), calls=%async_computation.3 | async-start | bytes 262144 | tf_op jit(solution)/shard_map/psum | solution.py:42
Sparse Core Ops, SparseCore 0:
  70.2 64.1 reduce-scatter.1
  136.6 20.4 all-reduce.1
